TPU v7x, 32 devices: a whole 2x2x4 slice. The times are simulated.
32 devices in a mesh: dp: 4 (over y, core), seq: 8 (over z, x).
Axes of the slice: x: 2, y: 2, z: 4, core: 2. Of those that a mesh axis runs over, the one named last changes fastest.
Arguments:
- tokens: bfloat16 [4, 24, 256, 1280], P('dp', 'seq'), may hold values from -6 to 6
- clip_ids: int32 [4, 24], P('dp'), may hold values from 0 to 5, never falling along the last dimension, each value on 1 to 12 neighbouring positions
- ln_gain: float32 [1280], replicated, may hold values from 0.1 to 1.9
- w_qkv: bfloat16 [1280, 1920], P(None, 'dp'), may hold values from -0.15625 to 0.15625
- w_out: bfloat16 [640, 1280], P(None, 'dp'), may hold values from -0.25 to 0.25
Outputs:
- output: bfloat16 [4, 24, 256, 1280], P('dp', 'seq')
Inputs may be any that keep to these rules, and one draw needn't show every extreme that they name: `clip_ids`: in each batch the clip numbers never fall along the frames, every clip number occurs, each clip covers 1 to 12 consecutive frames, and some clip covers exactly 12.
All inputs are finite; a program needn't handle non-finite values.
Results may differ from a plain program's by a relative error of at most 0.006.
Values may be sent and summed in bfloat16 or wider, within the bound.
A program may use at most 64 MiB of HBM per device.

v0:
```python
import math
import jax
import jax.numpy as jnp
from jax import lax
from jax.sharding import PartitionSpec as P

HS = 80
HEADS = 8
HD = 640
norm_eps = 1e-05


def layer_norm(block, ln_gain):
    values = block.astype(jnp.float32)
    center = jnp.mean(values, axis=-1, keepdims=True)
    spread = jnp.mean(jnp.square(values - center), axis=-1, keepdims=True)
    return ((values - center) * lax.rsqrt(spread + norm_eps) * ln_gain).astype(jnp.bfloat16)


def split_heads(projected):
    queries = (projected[:, :HD] * (1.0 / math.sqrt(HS))).astype(jnp.bfloat16)
    keys = projected[:, HD : 2 * HD].astype(jnp.bfloat16)
    values = projected[:, 2 * HD :].astype(jnp.bfloat16)
    return (queries, keys, values)


def attend(queries, keys, values, clip_row):
    scores = jnp.einsum("flhe,glhe->lhfg", queries, keys, preferred_element_type=jnp.float32)
    same_clip = clip_row[:, None] == clip_row[None, :]
    raised = jnp.where(same_clip, jnp.exp(scores), jnp.zeros_like(scores))
    attn_probs = (raised / jnp.sum(raised, axis=-1, keepdims=True)).astype(jnp.bfloat16)
    return jnp.einsum(
        "lhfg,glhe->flhe", attn_probs, values, preferred_element_type=jnp.float32
    ).astype(jnp.bfloat16)


def shards(tokens, clip_ids, ln_gain, w_qkv, w_out):
    width = tokens.shape[3]
    clip_row = clip_ids[0]
    frames = clip_row.shape[0]
    local_frames = tokens.shape[1]
    patches = tokens.shape[2]
    moved = lax.all_to_all(tokens, "seq", split_axis=2, concat_axis=1, tiled=True)
    places = moved.shape[2]
    normed = layer_norm(moved, ln_gain).reshape(frames * places, width)

    def column_block(piece, start):
        return jnp.dot(normed, piece, preferred_element_type=jnp.float32)

    queries, keys, values = split_heads(
        column_block(lax.all_gather(w_qkv, "dp", axis=1, tiled=True), jnp.int32(0))
    )
    head_shape = (frames, places, HEADS, HS)
    mixed = attend(
        queries.reshape(head_shape), keys.reshape(head_shape), values.reshape(head_shape), clip_row
    )
    mixed = lax.all_to_all(
        mixed.reshape(1, frames, places, HD), "seq", split_axis=1, concat_axis=2, tiled=True
    )
    row_count = local_frames * patches
    rows_in = mixed.reshape(row_count, HD)

    def column_block(piece, start):
        return jnp.dot(rows_in, piece, preferred_element_type=jnp.float32)

    update = column_block(lax.all_gather(w_out, "dp", axis=1, tiled=True), jnp.int32(0))
    summed = tokens.reshape(row_count, width).astype(jnp.float32) + update
    return summed.astype(jnp.bfloat16).reshape(tokens.shape)


def solution(mesh):
    placed = (P("dp", "seq", None, None), P("dp", None), P(), P(None, "dp"), P(None, "dp"))
    return jax.shard_map(
        shards, mesh=mesh, in_specs=placed, out_specs=P("dp", "seq", None, None), check_vma=False
    )
```

profile of v0, /device:TPU:0, one launch (start us, length us, event | category | flops | bytes accessed | tf_op | source)
XLA Modules:
  0.0 151.9 jit_solution(18149255715372341711)
XLA Ops:
  6.5 0.7 all-gather.3.cloned.1.call-update
  7.3 4.8 %copy.35 = bf16[1,3,256,1280]{3,1,0,2:T(4,128)(2,1)} copy(bf16[1,3,256,1280]{3,2,1,0:T(8,128)(2,1)} %param.5) | data formatting | bytes 3932160 | tf_op args[0]
  12.0 7.4 %all-to-all-start = ((bf16[1,3,256,1280]{3,1,0,2:T(4,128)(2,1)}), bf16[1,3,256,1280]{3,1,0,2:T(4,128)(2,1)S(1)}, u32[]{:S(2)}, u32[]{:S(2)}) async-start(bf16[1,3,256,1280]{3,1,0,2:T(4,128)(2,1)} %copy.35), calls=%async_computation | async-start | bytes 5242880 | tf_op jit(solution)/shard_map/all_to_all | solution.py:43
  19.5 0.7 all-gather.5.cloned.1.call-update
  20.3 58.6 %all-to-all-done = bf16[1,3,256,1280]{3,1,0,2:T(4,128)(2,1)S(1)} async-done(((bf16[1,3,256,1280]{3,1,0,2:T(4,128)(2,1)}), bf16[1,3,256,1280]{3,1,0,2:T(4,128)(2,1)S(1)}, u32[]{:S(2)}, u32[]{:S(2)}) %all-to-all-start) | async-done | bytes 1966112 | tf_op jit(solution)/shard_map/all_to_all | solution.py:43
  78.9 2.3 %convert_bitcast_fusion = (f32[1,8,3,32,1280]{4,3,1,2,0:T(8,128)}, bf16[1,3,256,1280]{3,2,1,0:T(8,128)(2,1)S(1)}) fusion(bf16[1,3,256,1280]{3,1,0,2:T(4,128)(2,1)S(1)} %all-to-all-done), kind=kLoop, calls=%fused_computation.1 | loop fusion | flops 983040 | bytes 7864320 | tf_op jit(solution)/shard_map/convert_element_type | solution.py:14
  81.2 0.3 fusion.5
  81.6 0.7 multiply_reduce_fusion
  82.3 0.1 rsqrt.12
  82.4 2.4 %copy.37 = f32[1,8,3,32,1280]{4,3,2,1,0:T(8,128)S(1)} copy(f32[1,8,3,32,1280]{4,3,1,2,0:T(8,128)} %get-tuple-element.5) | data formatting | bytes 7864320 | tf_op jit(solution)/shard_map/convert_element_type | solution.py:14
  84.9 0.6 fusion.2
  85.5 8.5 %fusion.18 = (bf16[768,1920]{1,0:T(8,128)(2,1)S(1)}, f32[768,1920]{1,0:T(8,128)}) fusion(bf16[768,1280]{1,0:T(8,128)(2,1)S(1)} %fusion.2, bf16[1280,1920]{0,1:T(8,128)(2,1)} %all-gather.3.cloned.1.call-done), kind=kOutput, calls=%fused_computation.27 | convolution fusion | flops 3776348160 | bytes 15728640 | tf_op jit(solution)/shard_map/dot_general | solution.py:48
  94.0 0.2 fusion.17
  94.2 1.6 %reshape.90 = bf16[24,32,8,80]{3,2,1,0:T(8,128)(2,1)S(1)} reshape(bf16[768,640]{1,0:T(8,128)(2,1)S(1)} %get-tuple-element.8) | data formatting | bytes 1966080 | tf_op jit(solution)/shard_map/reshape | solution.py:55
  95.8 1.7 %fusion.6 = bf16[768,640]{1,0:T(8,128)(2,1)S(1)} fusion(f32[768,1920]{1,0:T(8,128)} %get-tuple-element.10), kind=kLoop, calls=%fused_computation.13 | loop fusion | flops 983040 | bytes 2949120 | tf_op jit(solution)/shard_map/convert_element_type | solution.py:21
  97.5 2.5 %reshape.89 = bf16[24,32,8,80]{3,2,1,0:T(8,128)(2,1)} reshape(bf16[768,640]{1,0:T(8,128)(2,1)S(1)} %fusion.6) | data formatting | bytes 1966080 | tf_op jit(solution)/shard_map/reshape | solution.py:55
  100.0 5.7 %fusion.4 = (f32[32,8,24]{2,1,0:T(8,128)S(1)}, f32[32,8,24,24]{2,3,1,0:T(8,128)}) fusion(pred[24,24]{0,1:T(8,128)(4,1)S(1)} %broadcast_compare_fusion, bf16[24,32,8,80]{3,2,1,0:T(8,128)(2,1)S(1)} %reshape.90, bf16[24,32,8,80]{3,2,1,0:T(8,128)(2,1)} %reshape.89), kind=kOutput, calls=%fused_computation.10 | convolution fusion | flops 23881728 | bytes 2581056 | tf_op jit(solution)/shard_map/flhe,glhe->lhfg/dot_general | solution.py:28
  105.7 1.6 %reshape.88 = bf16[24,32,8,80]{3,2,1,0:T(8,128)(2,1)S(1)} reshape(bf16[768,640]{1,0:T(8,128)(2,1)S(1)} %get-tuple-element.7) | data formatting | bytes 1966080 | tf_op jit(solution)/shard_map/reshape | solution.py:55
  107.3 3.4 %fusion.13 = bf16[24,32,8,80]{3,0,2,1:T(8,128)(2,1)S(1)} fusion(f32[32,8,24,24]{2,3,1,0:T(8,128)} %get-tuple-element.12, f32[32,8,24]{2,1,0:T(8,128)S(1)} %get-tuple-element.11, pred[24,24]{0,1:T(8,128)(4,1)S(1)} %broadcast_compare_fusion, bf16[24,32,8,80]{3,2,1,0:T(8,128)(2,1)S(1)} %reshape.88), kind=kOutput, calls=%fused_computation.21 | convolution fusion | flops 24526848 | bytes 2581056 | tf_op jit(solution)/shard_map/lhfg,glhe->flhe/dot_general | solution.py:32
  110.7 0.3 copy.44
  111.1 1.2 reshape.91
  112.3 28.2 %all_to_all.24 = bf16[1,24,32,640]{3,2,0,1:T(8,128)(2,1)S(1)} all-to-all(bf16[1,24,32,640]{3,2,0,1:T(8,128)(2,1)S(1)} %bitcast.36), channel_id=1, replica_groups=mesh['dp'=4,'seq'=8] {'seq'}, dimensions={1} | all-to-all | bytes 1966080 | tf_op jit(solution)/shard_map/all_to_all | solution.py:57
  140.5 0.1 copy.46
  140.6 4.4 %fusion.3 = bf16[768,1280]{1,0:T(8,128)(2,1)} fusion(bf16[768,640]{1,0:T(8,128)(2,1)S(1)} %bitcast.39, bf16[640,1280]{0,1:T(8,128)(2,1)} %all-gather.5.cloned.1.call-done, bf16[768,1280]{1,0:T(8,128)(2,1)S(1)} %bitcast.38), kind=kOutput, calls=%fused_computation.7 | convolution fusion | flops 1261240320 | bytes 6553600 | tf_op jit(solution)/shard_map/dot_general | solution.py:64
  (16 shorter events, 0.3 us)
Async XLA Ops:
  6.5 78.9 %all-gather.3.cloned.1.call-start = ((), (), s32[]{:S(2)}) async-start(), calls=%async_computation.2 | async-start | bytes 6144000 | tf_op jit(solution)/shard_map/all_gather | solution.py:51
  12.0 8.2 %copy-start.2 = (s32[1,24]{1,0:T(1,128)S(1)}, s32[1,24]{1,0:T(1,128)}, u32[]{:S(2)}) copy-start(s32[1,24]{1,0:T(1,128)} %param.6) | copy-start | bytes 292
  12.0 66.9 %all-to-all-start = ((bf16[1,3,256,1280]{3,1,0,2:T(4,128)(2,1)}), bf16[1,3,256,1280]{3,1,0,2:T(4,128)(2,1)S(1)}, u32[]{:S(2)}, u32[]{:S(2)}) async-start(bf16[1,3,256,1280]{3,1,0,2:T(4,128)(2,1)} %copy.35), calls=%async_computation | async-start | bytes 5242880 | tf_op jit(solution)/shard_map/all_to_all | solution.py:43
  19.4 121.2 %all-gather.5.cloned.1.call-start = ((), (), s32[]{:S(2)}) async-start(), calls=%async_computation.3 | async-start | bytes 2048000 | tf_op jit(solution)/shard_map/all_gather | solution.py:66
  82.4 2.4 %copy-start.1 = (f32[1280]{0:T(1024)S(1)}, f32[1280]{0:T(1024)}, u32[]{:S(2)}) copy-start(f32[1280]{0:T(1024)} %param.7) | copy-start | bytes 15364
  112.3 28.3 %copy-start = (bf16[1,3,256,1280]{3,2,1,0:T(8,128)(2,1)S(1)}, bf16[1,3,256,1280]{3,2,1,0:T(8,128)(2,1)}, u32[]{:S(2)}) copy-start(bf16[1,3,256,1280]{3,2,1,0:T(8,128)(2,1)} %param.5) | copy-start | bytes 5898244
Sparse Core Ops, SparseCore 0:
  8.9 41.2 all-gather.2
  51.8 19.9 all-gather.4
where the time goes:
time: 152 us
  waiting for transfers between devices  60.1 us (40%)
  blocking collectives  28.2 us (19%)
  matrix products  22 us (14%)
  local copies, waits for them, and re-layouts  14.9 us (10%)
  between operations  13.6 us (9%)
  starting transfers between devices  7.45 us (5%)
  other arithmetic  5.69 us (4%)
    all_to_all x1, waiting for transfers between devices, shards(): lax.all_to_all(tokens, 'seq', split_axis=2, concat_axis=1, tiled=True)  58.6 us
    all_to_all x1, blocking collectives, shards(): lax.all_to_all(mixed.reshape(1, frames, places, HD), 'seq', split_axis=1,...  28.2 us
    dot_general x1, matrix products, column_block(): return jnp.dot(normed, piece, preferred_element_type=jnp.float32)  8.52 us
    all_to_all x1, starting transfers between devices, shards(): lax.all_to_all(tokens, 'seq', split_axis=2, concat_axis=1, tiled=True)  7.41 us
    dot_general x1, matrix products, attend(): jnp.einsum('flhe,glhe->lhfg', queries, keys, preferred_element_type=jnp.f...  5.69 us
    unnamed x7, local copies, waits for them, and re-layouts  4.77 us
    dot_general x1, matrix products, column_block(): return jnp.dot(rows_in, piece, preferred_element_type=jnp.float32)  4.43 us
    dot_general x1, matrix products, attend(): jnp.einsum('lhfg,glhe->flhe', attn_probs, values, preferred_element_type=...  3.4 us
  transfers between devices with their start and end apart: 3, of which 1 were waited for; matrix products, arithmetic and copies ran while one was open for 25% of the time, Pallas kernels for 0%

commit v1 on v0

--- a/solution.py
+++ b/solution.py
@@ -8,6 +8,30 @@
 HEADS = 8
 HD = 640
 norm_eps = 1e-05
+
+
+def cut_along(x, dim, peers):
+    before, after = (x.shape[:dim], x.shape[dim + 1 :])
+    return jnp.moveaxis(x.reshape(*before, peers, -1, *after), dim, 0)
+
+
+def joined_along(blocks, dim):
+    lengths = list(blocks.shape[1:])
+    lengths[dim] *= blocks.shape[0]
+    return jnp.moveaxis(blocks, 0, dim).reshape(lengths)
+
+
+def rotated_exchange(x, axis, split_dim, concat_dim):
+    devices, mine = (lax.axis_size(axis), lax.axis_index(axis))
+    parts = cut_along(x, split_dim, devices)
+    finished = [parts[mine]]
+    for hop in range(1, devices):
+        sent = parts[(mine + hop) % devices]
+        finished.append(
+            lax.ppermute(sent, axis, [(i, (i + hop) % devices) for i in range(devices)])
+        )
+    parts = jnp.stack(finished)[(mine - jnp.arange(devices)) % devices]
+    return joined_along(parts, concat_dim)
 
 
 def layer_norm(block, ln_gain):
@@ -54,9 +78,7 @@
     mixed = attend(
         queries.reshape(head_shape), keys.reshape(head_shape), values.reshape(head_shape), clip_row
     )
-    mixed = lax.all_to_all(
-        mixed.reshape(1, frames, places, HD), "seq", split_axis=1, concat_axis=2, tiled=True
-    )
+    mixed = rotated_exchange(mixed.reshape(1, frames, places, HD), "seq", 1, 2)
     row_count = local_frames * patches
     rows_in = mixed.reshape(row_count, HD)
 

time: 152 us -> 149 us (0.980)
  the two profiles are of different devices: /device:TPU:0 before, /device:TPU:15 now
where the time goes in v1:
time: 149 us
  waiting for transfers between devices  75.7 us (51%)
  matrix products  19.6 us (13%)
  local copies, waits for them, and re-layouts  18.7 us (13%)
  starting transfers between devices  15.1 us (10%)
  between operations  13.7 us (9%)
  other arithmetic  5.95 us (4%)
    all_to_all x1, waiting for transfers between devices, shards(): lax.all_to_all(tokens, 'seq', split_axis=2, concat_axis=1, tiled=True)  56 us
    ppermute x7, waiting for transfers between devices, rotated_exchange(): lax.ppermute(sent, axis, [(i, (i + hop) % devices) for i in range(devices)])  18.2 us
    ppermute x7, starting transfers between devices, rotated_exchange(): lax.ppermute(sent, axis, [(i, (i + hop) % devices) for i in range(devices)])  9.33 us
    dot_general x1, matrix products, column_block(): return jnp.dot(normed, piece, preferred_element_type=jnp.float32)  8.5 us
    unnamed x13, local copies, waits for them, and re-layouts  5.8 us
    all_to_all x1, starting transfers between devices, shards(): lax.all_to_all(tokens, 'seq', split_axis=2, concat_axis=1, tiled=True)  5.79 us
    dot_general x1, matrix products, column_block(): return jnp.dot(rows_in, piece, preferred_element_type=jnp.float32)  5.04 us
    dot_general x1, matrix products, attend(): jnp.einsum('flhe,glhe->lhfg', queries, keys, preferred_element_type=jnp.f...  4.53 us
  transfers between devices with their start and end apart: 10, of which 5 were waited for; matrix products, arithmetic and copies ran while one was open for 26% of the time, Pallas kernels for 0%

profile of v1, /device:TPU:15, one launch (start us, length us, event | category | flops | bytes accessed | tf_op | source)
XLA Modules:
  0.0 148.7 jit_solution(8083725729783395908)
XLA Ops:
  7.3 4.7 %copy.24 = bf16[1,3,256,1280]{3,1,0,2:T(4,128)(2,1)} copy(bf16[1,3,256,1280]{3,2,1,0:T(8,128)(2,1)} %param.5) | data formatting | bytes 3932160 | tf_op args[0]
  12.0 5.8 %all-to-all-start = ((bf16[1,3,256,1280]{3,1,0,2:T(4,128)(2,1)}), bf16[1,3,256,1280]{3,1,0,2:T(4,128)(2,1)S(1)}, u32[]{:S(2)}, u32[]{:S(2)}) async-start(bf16[1,3,256,1280]{3,1,0,2:T(4,128)(2,1)} %copy.24), calls=%async_computation | async-start | bytes 5242880 | tf_op jit(solution)/shard_map/all_to_all | solution.py:67
  18.7 56.0 %all-to-all-done = bf16[1,3,256,1280]{3,1,0,2:T(4,128)(2,1)S(1)} async-done(((bf16[1,3,256,1280]{3,1,0,2:T(4,128)(2,1)}), bf16[1,3,256,1280]{3,1,0,2:T(4,128)(2,1)S(1)}, u32[]{:S(2)}, u32[]{:S(2)}) %all-to-all-start) | async-done | bytes 1966112 | tf_op jit(solution)/shard_map/all_to_all | solution.py:67
  76.2 2.1 %copy.26 = f32[1,8,3,32,1280]{4,3,2,1,0:T(8,128)} copy(f32[1,8,3,32,1280]{4,3,1,2,0:T(8,128)S(1)} %get-tuple-element.5) | data formatting | bytes 7864320 | tf_op jit(solution)/shard_map/convert_element_type | solution.py:38
  78.6 2.7 %fusion.2 = bf16[768,1280]{1,0:T(8,128)(2,1)S(1)} fusion(f32[1,8,3,32,1280]{4,3,2,1,0:T(8,128)} %copy.26, f32[1280]{0:T(1024)S(1)} %copy-done.1, f32[768]{0:T(1024)S(1)} %rsqrt.12, f32[768]{0:T(1024)S(1)} %div.17), kind=kLoop, calls=%fused_computation.6 | loop fusion | flops 3932160 | bytes 5909504 | tf_op jit(solution)/shard_map/convert_element_type | solution.py:41
  81.3 8.5 %fusion.20 = (bf16[768,1920]{1,0:T(8,128)(2,1)S(1)}, f32[768,1920]{1,0:T(8,128)}) fusion(bf16[768,1280]{1,0:T(8,128)(2,1)S(1)} %fusion.2, bf16[1280,1920]{0,1:T(8,128)(2,1)} %all-gather.3.cloned.1.call-done), kind=kOutput, calls=%fused_computation.50 | convolution fusion | flops 3776348160 | bytes 15728640 | tf_op jit(solution)/shard_map/dot_general | solution.py:72
  89.9 2.5 %reshape.132 = bf16[24,32,8,80]{3,2,1,0:T(8,128)(2,1)} reshape(bf16[768,640]{1,0:T(8,128)(2,1)S(1)} %get-tuple-element.8) | data formatting | bytes 1966080 | tf_op jit(solution)/shard_map/reshape | solution.py:79
  92.4 1.7 %fusion.6 = bf16[768,640]{1,0:T(8,128)(2,1)S(1)} fusion(f32[768,1920]{1,0:T(8,128)} %get-tuple-element.18), kind=kLoop, calls=%fused_computation.14 | loop fusion | flops 983040 | bytes 2949120 | tf_op jit(solution)/shard_map/convert_element_type | solution.py:45
  94.2 2.5 %reshape.131 = bf16[24,32,8,80]{3,2,1,0:T(8,128)(2,1)} reshape(bf16[768,640]{1,0:T(8,128)(2,1)S(1)} %fusion.6) | data formatting | bytes 1966080 | tf_op jit(solution)/shard_map/reshape | solution.py:79
  96.7 1.6 %reshape.130 = bf16[24,32,8,80]{3,2,1,0:T(8,128)(2,1)S(1)} reshape(bf16[768,640]{1,0:T(8,128)(2,1)S(1)} %get-tuple-element.7) | data formatting | bytes 1966080 | tf_op jit(solution)/shard_map/reshape | solution.py:79
  98.3 4.5 %fusion.4 = (f32[32,8,24]{2,1,0:T(8,128)S(1)}, f32[32,8,24,24]{2,3,1,0:T(8,128)S(1)}) fusion(pred[24,24]{0,1:T(8,128)(4,1)S(1)} %broadcast_compare_fusion, bf16[24,32,8,80]{3,2,1,0:T(8,128)(2,1)} %reshape.132, bf16[24,32,8,80]{3,2,1,0:T(8,128)(2,1)} %reshape.131), kind=kOutput, calls=%fused_computation.11 | convolution fusion | flops 23881728 | bytes 2581056 | tf_op jit(solution)/shard_map/flhe,glhe->lhfg/dot_general | solution.py:52
  102.8 1.5 %fusion.13 = bf16[24,32,8,80]{3,0,2,1:T(8,128)(2,1)S(1)} fusion(f32[32,8,24,24]{2,3,1,0:T(8,128)S(1)} %get-tuple-element.20, f32[32,8,24]{2,1,0:T(8,128)S(1)} %get-tuple-element.19, pred[24,24]{0,1:T(8,128)(4,1)S(1)} %broadcast_compare_fusion, bf16[24,32,8,80]{3,2,1,0:T(8,128)(2,1)S(1)} %reshape.130), kind=kOutput, calls=%fused_computation.22 | convolution fusion | flops 24526848 | bytes 2581056 | tf_op jit(solution)/shard_map/lhfg,glhe->flhe/dot_general | solution.py:56
  104.7 1.2 transpose_reshape_reshape.3
  106.2 4.1 %collective-permute-start.1 = (bf16[1,3,32,640]{3,2,1,0:T(8,128)(2,1)S(1)}, bf16[1,3,32,640]{3,2,1,0:T(8,128)(2,1)S(1)}, u32[]{:S(2)}, u32[]{:S(2)}) collective-permute-start(bf16[1,3,32,640]{3,2,1,0:T(8,128)(2,1)S(1)} %get-tuple-element.14), channel_id=1, source_target_pairs={{0,2},{1,3},{2,4},{3,5},{4,6},{5,7},{6,0},{7,1},{8,10},{9,11},{10,... | collective-permute-start | bytes 368648 | tf_op jit(solution)/shard_map/ppermute | solution.py:31
  110.3 1.3 collective-permute-start.2
  111.6 1.4 collective-permute-start.4
  112.9 1.9 %collective-permute-start.5 = (bf16[1,3,32,640]{3,2,1,0:T(8,128)(2,1)S(1)}, bf16[1,3,32,640]{3,2,1,0:T(8,128)(2,1)S(1)}, u32[]{:S(2)}, u32[]{:S(2)}) collective-permute-start(bf16[1,3,32,640]{3,2,1,0:T(8,128)(2,1)S(1)} %get-tuple-element.10), channel_id=1, source_target_pairs={{0,6},{1,7},{2,0},{3,1},{4,2},{5,3},{6,4},{7,5},{8,14},{9,15},{10,... | collective-permute-start | bytes 368648 | tf_op jit(solution)/shard_map/ppermute | solution.py:31
  115.5 9.9 %collective-permute-done.2 = bf16[1,3,32,640]{3,2,1,0:T(8,128)(2,1)S(1)} collective-permute-done((bf16[1,3,32,640]{3,2,1,0:T(8,128)(2,1)S(1)}, bf16[1,3,32,640]{3,2,1,0:T(8,128)(2,1)S(1)}, u32[]{:S(2)}, u32[]{:S(2)}) %collective-permute-start.2) | collective-permute-done | bytes 122912 | tf_op jit(solution)/shard_map/ppermute | solution.py:31
  125.4 2.6 %collective-permute-done.3 = bf16[1,3,32,640]{3,2,1,0:T(8,128)(2,1)S(1)} collective-permute-done((bf16[1,3,32,640]{3,2,1,0:T(8,128)(2,1)S(1)}, bf16[1,3,32,640]{3,2,1,0:T(8,128)(2,1)S(1)}, u32[]{:S(2)}, u32[]{:S(2)}) %collective-permute-start.3) | collective-permute-done | bytes 122912 | tf_op jit(solution)/shard_map/ppermute | solution.py:31
  128.1 4.1 %collective-permute-done.5 = bf16[1,3,32,640]{3,2,1,0:T(8,128)(2,1)S(1)} collective-permute-done((bf16[1,3,32,640]{3,2,1,0:T(8,128)(2,1)S(1)}, bf16[1,3,32,640]{3,2,1,0:T(8,128)(2,1)S(1)}, u32[]{:S(2)}, u32[]{:S(2)}) %collective-permute-start.5) | collective-permute-done | bytes 122912 | tf_op jit(solution)/shard_map/ppermute | solution.py:31
  132.2 1.6 %collective-permute-done.6 = bf16[1,3,32,640]{3,2,1,0:T(8,128)(2,1)S(1)} collective-permute-done((bf16[1,3,32,640]{3,2,1,0:T(8,128)(2,1)S(1)}, bf16[1,3,32,640]{3,2,1,0:T(8,128)(2,1)S(1)}, u32[]{:S(2)}, u32[]{:S(2)}) %collective-permute-start.6) | collective-permute-done | bytes 122912 | tf_op jit(solution)/shard_map/ppermute | solution.py:31
  133.8 0.9 copy-done
  134.8 1.9 %gather_fusion = bf16[8,3,32,640]{3,2,1,0:T(8,128)(2,1)S(1)} fusion(bf16[8,3,32,640]{3,2,1,0:T(8,128)(2,1)} %bitcast.68, s32[1024]{0:T(1024)S(1)} %pad_clamp_fusion), kind=kCustom, calls=%fused_computation | custom fusion | bytes 1966112 | tf_op jit(solution)/shard_map/gather | solution.py:33
  136.9 5.0 %fusion.3 = bf16[768,1280]{1,0:T(8,128)(2,1)} fusion(bf16[768,640]{1,0:T(8,128)(2,1)S(1)} %bitcast.69, bf16[640,1280]{0,1:T(8,128)(2,1)} %all-gather.5.cloned.1.call-done, bf16[768,1280]{1,0:T(8,128)(2,1)} %bitcast.67), kind=kOutput, calls=%fused_computation.8 | convolution fusion | flops 1261240320 | bytes 6553600 | tf_op jit(solution)/shard_map/dot_general | solution.py:86
  (40 shorter events, 4.8 us)
Async XLA Ops:
  6.5 74.7 %all-gather.3.cloned.1.call-start = ((), (), s32[]{:S(2)}) async-start(), calls=%async_computation.1 | async-start | bytes 6144000 | tf_op jit(solution)/shard_map/all_gather | solution.py:75
  12.0 6.6 %copy-start.2 = (s32[1,24]{1,0:T(1,128)S(1)}, s32[1,24]{1,0:T(1,128)}, u32[]{:S(2)}) copy-start(s32[1,24]{1,0:T(1,128)} %param.6) | copy-start | bytes 292
  12.0 62.7 %all-to-all-start = ((bf16[1,3,256,1280]{3,1,0,2:T(4,128)(2,1)}), bf16[1,3,256,1280]{3,1,0,2:T(4,128)(2,1)S(1)}, u32[]{:S(2)}, u32[]{:S(2)}) async-start(bf16[1,3,256,1280]{3,1,0,2:T(4,128)(2,1)} %copy.24), calls=%async_computation | async-start | bytes 5242880 | tf_op jit(solution)/shard_map/all_to_all | solution.py:67
  17.8 119.1 %all-gather.5.cloned.1.call-start = ((), (), s32[]{:S(2)}) async-start(), calls=%async_computation.2 | async-start | bytes 2048000 | tf_op jit(solution)/shard_map/all_gather | solution.py:88
  76.2 2.3 %copy-start.1 = (f32[1280]{0:T(1024)S(1)}, f32[1280]{0:T(1024)}, u32[]{:S(2)}) copy-start(f32[1280]{0:T(1024)} %param.7) | copy-start | bytes 15364
  106.1 6.9 %collective-permute-start = (bf16[1,3,32,640]{3,2,1,0:T(8,128)(2,1)S(1)}, bf16[1,3,32,640]{3,2,1,0:T(8,128)(2,1)S(1)}, u32[]{:S(2)}, u32[]{:S(2)}) collective-permute-start(bf16[1,3,32,640]{3,2,1,0:T(8,128)(2,1)S(1)} %get-tuple-element.15), channel_id=1, source_target_pairs={{0,1},{1,2},{2,3},{3,4},{4,5},{5,6},{6,7},{7,0},{8,9},{9,10},{10,1... | collective-permute-start | bytes 368648 | tf_op jit(solution)/shard_map/ppermute | solution.py:31
  106.2 8.7 %collective-permute-start.1 = (bf16[1,3,32,640]{3,2,1,0:T(8,128)(2,1)S(1)}, bf16[1,3,32,640]{3,2,1,0:T(8,128)(2,1)S(1)}, u32[]{:S(2)}, u32[]{:S(2)}) collective-permute-start(bf16[1,3,32,640]{3,2,1,0:T(8,128)(2,1)S(1)} %get-tuple-element.14), channel_id=1, source_target_pairs={{0,2},{1,3},{2,4},{3,5},{4,6},{5,7},{6,0},{7,1},{8,10},{9,11},{10,... | collective-permute-start | bytes 368648 | tf_op jit(solution)/shard_map/ppermute | solution.py:31
  110.3 15.1 %collective-permute-start.2 = (bf16[1,3,32,640]{3,2,1,0:T(8,128)(2,1)S(1)}, bf16[1,3,32,640]{3,2,1,0:T(8,128)(2,1)S(1)}, u32[]{:S(2)}, u32[]{:S(2)}) collective-permute-start(bf16[1,3,32,640]{3,2,1,0:T(8,128)(2,1)S(1)} %get-tuple-element.13), channel_id=1, source_target_pairs={{0,3},{1,4},{2,5},{3,6},{4,7},{5,0},{6,1},{7,2},{8,11},{9,12},{10,... | collective-permute-start | bytes 368648 | tf_op jit(solution)/shard_map/ppermute | solution.py:31
  111.6 16.5 %collective-permute-start.3 = (bf16[1,3,32,640]{3,2,1,0:T(8,128)(2,1)S(1)}, bf16[1,3,32,640]{3,2,1,0:T(8,128)(2,1)S(1)}, u32[]{:S(2)}, u32[]{:S(2)}) collective-permute-start(bf16[1,3,32,640]{3,2,1,0:T(8,128)(2,1)S(1)} %get-tuple-element.12), channel_id=1, source_target_pairs={{0,4},{1,5},{2,6},{3,7},{4,0},{5,1},{6,2},{7,3},{8,12},{9,13},{10,... | collective-permute-start | bytes 368648 | tf_op jit(solution)/shard_map/ppermute | solution.py:31
  111.6 16.5 %collective-permute-start.4 = (bf16[1,3,32,640]{3,2,1,0:T(8,128)(2,1)S(1)}, bf16[1,3,32,640]{3,2,1,0:T(8,128)(2,1)S(1)}, u32[]{:S(2)}, u32[]{:S(2)}) collective-permute-start(bf16[1,3,32,640]{3,2,1,0:T(8,128)(2,1)S(1)} %get-tuple-element.11), channel_id=1, source_target_pairs={{0,5},{1,6},{2,7},{3,0},{4,1},{5,2},{6,3},{7,4},{8,13},{9,14},{10,... | collective-permute-start | bytes 368648 | tf_op jit(solution)/shard_map/ppermute | solution.py:31
  112.9 19.3 %collective-permute-start.5 = (bf16[1,3,32,640]{3,2,1,0:T(8,128)(2,1)S(1)}, bf16[1,3,32,640]{3,2,1,0:T(8,128)(2,1)S(1)}, u32[]{:S(2)}, u32[]{:S(2)}) collective-permute-start(bf16[1,3,32,640]{3,2,1,0:T(8,128)(2,1)S(1)} %get-tuple-element.10), channel_id=1, source_target_pairs={{0,6},{1,7},{2,0},{3,1},{4,2},{5,3},{6,4},{7,5},{8,14},{9,15},{10,... | collective-permute-start | bytes 368648 | tf_op jit(solution)/shard_map/ppermute | solution.py:31
  114.8 19.0 %collective-permute-start.6 = (bf16[1,3,32,640]{3,2,1,0:T(8,128)(2,1)S(1)}, bf16[1,3,32,640]{3,2,1,0:T(8,128)(2,1)S(1)}, u32[]{:S(2)}, u32[]{:S(2)}) collective-permute-start(bf16[1,3,32,640]{3,2,1,0:T(8,128)(2,1)S(1)} %get-tuple-element.9), channel_id=1, source_target_pairs={{0,7},{1,0},{2,1},{3,2},{4,3},{5,4},{6,5},{7,6},{8,15},{9,8},{10,9... | collective-permute-start | bytes 368648 | tf_op jit(solution)/shard_map/ppermute | solution.py:31
  133.8 0.9 copy-start
Sparse Core Ops, SparseCore 0:
  8.9 39.1 all-gather.2
  49.6 19.9 all-gather.4
